TPU v7x, 128 devices: a whole 4x4x4 slice. The times are simulated.
128 devices in a mesh: blk: 128 (over z, x, y, core).
Axes of the slice: x: 4, y: 4, z: 4, core: 2. Of those that a mesh axis runs over, the one named last changes fastest.
Arguments:
- state: float32 [4, 2048, 128, 256], P(None, 'blk'), may hold values from -6 to 6
- sample_cell: int32 [65536], P('blk'), may hold values from 0 to 491262, as said below
- sample_frac: float32 [3, 65536], P(None, 'blk'), may hold values from 0 to 1
- sample_owner: int32 [65536, 1], P('blk'), may hold values from 0 to 127; in each aligned block of 512 rows (0 to 511, 512 to 1023, ...) at most 8 rows name the same one
- face_angles: float32 [2, 131072], P(None, 'blk'), may hold values from -3.140625 to 3.140625
- face_height: float32 [131072], P('blk'), may hold values from 0.05 to 0.5
- wall_temp: float32 [131072], P('blk'), may hold values from -6 to 6
- face_visc: float32 [131072], P('blk'), may hold values from 0.005 to 0.05
Outputs:
- final_state: float32 [4, 2048, 128, 256], P(None, 'blk')
- wall_flux: float32 [4, 65536], P(None, 'blk')
Inputs may be any that keep to these rules, and one draw needn't show every extreme that they name: `sample_cell`: index i * 128 * 256 + j * 256 + k with i < 15, j < 127, k < 255, so that the whole block lies in the partition. `sample_owner`: among the 512 exchange points of one partition no owner is named more than 8 times, a bound that some block reaches.
All inputs are finite; a program needn't handle non-finite values.
Results may differ from a plain program's by a relative error of at most 0.0003.
Values sent between devices are 32-bit elements; how exact they have to be, the bound alone decides.
No kernel may reach another device: no remote copies, remote signals or barrier semaphores. Data moves between devices by JAX's collectives and lax.ppermute only.
A program may use at most 128 MiB of HBM per device.

v0:
```python
import jax
import jax.numpy as jnp
from jax import lax
from jax.sharding import PartitionSpec as P

NPTS = 64
NEWTON = 3
time_step = 0.1
grid_viscosity = 0.2
karman = 0.41
prandtl = 0.72
turb_prandtl = 0.9
speed_floor = 0.5


def extended(cells, sides, width):
    for axis, dim in sides:
        count = lax.axis_size(axis)
        head = lax.slice_in_dim(cells, 0, width, axis=dim)
        tail = lax.slice_in_dim(cells, cells.shape[dim] - width, cells.shape[dim], axis=dim)
        cells = jnp.concatenate(
            [
                lax.ppermute(tail, axis, [(i, (i + 1) % count) for i in range(count)]),
                cells,
                lax.ppermute(head, axis, [((i + 1) % count, i) for i in range(count)]),
            ],
            axis=dim,
        )
    return cells


def transport(padded):
    center = padded[:, 1:-1]
    velocity = center[0:3]
    framed = jnp.pad(center, ((0, 0), (0, 0), (1, 1), (1, 1)))
    east_side = padded[:, 2:]
    west_side = padded[:, :-2]
    north_side = framed[:, :, 2:, 1:-1]
    south_side = framed[:, :, :-2, 1:-1]
    upper_side = framed[:, :, 1:-1, 2:]
    lower_side = framed[:, :, 1:-1, :-2]
    advect = (
        velocity[0] * (east_side - west_side)
        + velocity[1] * (north_side - south_side)
        + velocity[2] * (upper_side - lower_side)
    )
    spread = (
        east_side + west_side + north_side + south_side + upper_side + lower_side - 6.0 * center
    )
    return -0.5 * advect + grid_viscosity * spread


def with_rims(field):
    return extended(field, (("blk", 1),), 1)


def corner_factor(fraction, upper_flag):
    if upper_flag:
        return fraction
    return 1.0 - fraction


def sample_lines(middle, sample_cell, sample_frac):
    span_cells = middle.shape[2]
    line_cells = middle.shape[3]
    points = sample_cell.shape[0]
    lines = middle.reshape(4, -1, line_cells)
    base_line = sample_cell // line_cells
    offset = sample_cell - base_line * line_cells
    line_ids = []
    plane_weights = []
    for step_x in (0, 1):
        for step_y in (0, 1):
            line_ids.append(base_line + step_x * span_cells + step_y)
            plane_weights.append(
                corner_factor(sample_frac[0], step_x) * corner_factor(sample_frac[1], step_y)
            )
    line_ids = jnp.stack(line_ids).reshape(-1)
    plane_weights = jnp.stack(plane_weights)
    picked = jnp.take(lines, line_ids, axis=1).reshape(4, 4, points, line_cells)
    along = lax.broadcasted_iota(jnp.int32, (points, line_cells), 1)
    lower_hit = (along == offset[:, None]).astype(jnp.float32)
    upper_hit = (along == offset[:, None] + 1).astype(jnp.float32)
    depth_weights = (
        lower_hit * (1.0 - sample_frac[2])[:, None] + upper_hit * sample_frac[2][:, None]
    )
    along_line = jnp.sum(picked * depth_weights[None, None], axis=3)
    return jnp.sum(along_line * plane_weights[None], axis=1)


def slot_index(owners, groups, capacity):
    onehot = (owners[:, None] == jnp.arange(groups, dtype=jnp.int32)[None, :]).astype(jnp.int32)
    before = jnp.cumsum(onehot, axis=0) - onehot
    position = jnp.sum(before * onehot, axis=1)
    return owners * capacity + position


def pick_slots(table, slot_table):
    return lax.dot_general(
        table,
        slot_table,
        (((1,), (1,)), ((), ())),
        precision=lax.Precision.HIGHEST,
        preferred_element_type=jnp.float32,
    )


def wall_model(sample, angles, height, wall_temp, viscosity):
    normal = jnp.stack(
        [
            jnp.sin(angles[0]) * jnp.cos(angles[1]),
            jnp.sin(angles[0]) * jnp.sin(angles[1]),
            jnp.cos(angles[0]),
        ]
    )
    normal_speed = jnp.sum(sample[0:3] * normal, axis=0)
    tangent = sample[0:3] - normal_speed[None] * normal
    tangent_speed = jnp.maximum(jnp.sqrt(jnp.sum(tangent * tangent, axis=0)), speed_floor)
    direction = tangent / tangent_speed[None]
    ladder = (jnp.arange(NPTS, dtype=jnp.float32) + 0.5) / NPTS
    heights = height[None] * (ladder * ladder)[:, None]
    quad_weights = height[None] * (2.0 * ladder / NPTS)[:, None]
    friction = jnp.sqrt(viscosity * tangent_speed / height)
    for newton_step in range(NEWTON):
        eddy_visc = viscosity[None] + karman * heights * friction[None]
        inverse_sum = jnp.sum(quad_weights / eddy_visc, axis=0)
        slope_sum = jnp.sum(quad_weights * karman * heights / (eddy_visc * eddy_visc), axis=0)
        residual = friction * friction * inverse_sum - tangent_speed
        derivative = 2.0 * friction * inverse_sum - friction * friction * slope_sum
        friction = friction - residual / derivative
    conduct = viscosity[None] / prandtl + karman * heights * friction[None] / turb_prandtl
    resist = jnp.sum(quad_weights / conduct, axis=0)
    heat_flux = (sample[3] - wall_temp) / resist
    stress = (friction * friction)[None] * direction
    return jnp.concatenate([stress, heat_flux[None]], axis=0)


def on_device(
    state, sample_cell, sample_frac, sample_owner, face_angles, face_height, wall_temp, face_visc
):
    groups = lax.axis_size("blk")
    capacity = face_height.shape[0] // groups
    middle = state + time_step * transport(with_rims(state))
    final_state = 0.5 * state + 0.5 * (middle + time_step * transport(with_rims(middle)))
    sampled = sample_lines(middle, sample_cell, sample_frac)
    slots = slot_index(sample_owner[:, 0], groups, capacity)
    slot_table = (slots[:, None] == jnp.arange(groups * capacity, dtype=jnp.int32)[None, :]).astype(
        jnp.float32
    )
    outgoing = jnp.dot(
        sampled, slot_table, precision=lax.Precision.HIGHEST, preferred_element_type=jnp.float32
    )
    incoming = lax.all_to_all(outgoing, "blk", split_axis=1, concat_axis=1, tiled=True)
    solved = wall_model(incoming, face_angles, face_height, wall_temp, face_visc)
    returned = lax.all_to_all(solved, "blk", split_axis=1, concat_axis=1, tiled=True)
    wall_flux = pick_slots(returned, slot_table)
    return (final_state, wall_flux)


def solution(mesh):
    placed = (
        P(None, "blk", None, None),
        P("blk"),
        P(None, "blk"),
        P("blk", None),
        P(None, "blk"),
        P("blk"),
        P("blk"),
        P("blk"),
    )
    return jax.shard_map(
        on_device,
        mesh=mesh,
        in_specs=placed,
        out_specs=(P(None, "blk", None, None), P(None, "blk")),
        check_vma=False,
    )
```

profile of v0, /device:TPU:1, one launch (start us, length us, event | category | flops | bytes accessed | tf_op | source)
XLA Modules:
  0.0 188.3 jit_solution(6805822651793586209)
XLA Ops:
  0.6 2.3 %fusion.37 = (f32[4,1,128,256]{3,2,1,0:T(8,128)}, f32[4,1,128,256]{3,2,1,0:T(8,128)}) fusion(f32[4,16,128,256]{3,2,1,0:T(8,128)} %param.8), kind=kLoop, calls=%fused_computation.128 | loop fusion | bytes 2097152 | tf_op jit(solution)/shard_map/slice | solution.py:20
  2.9 1.4 collective-permute-start
  4.3 1.3 collective-permute-start.1
  6.4 0.8 subtract_multiply_fusion.1
  7.2 0.8 copy.62
  8.3 0.9 fusion.25
  9.9 1.0 cosine_reduce_fusion
  11.7 5.6 %slice_bitcast_fusion.5 = (f32[16,128,256]{2,1,0:T(8,128)S(1)}, f32[16,128,256]{2,1,0:T(8,128)}, f32[16,128,256]{2,1,0:T(8,128)}) fusion(f32[4,16,128,256]{3,2,1,0:T(8,128)} %param.8), kind=kLoop, calls=%fused_computation.22 | loop fusion | bytes 12582912 | tf_op jit(solution)/shard_map/mul | solution.py:43
  17.3 26.2 %multiply_add_fusion = f32[4,16,128,256]{3,2,1,0:T(8,128)} fusion(f32[4,16,128,256]{3,2,1,0:T(8,128)} %param.8, f32[4,1,128,256]{3,2,1,0:T(8,128)S(1)} %collective-permute-done, f32[4,1,128,256]{3,2,1,0:T(8,128)} %collective-permute-done.1, f32[16,128,256]{2,1,0:T(8,128)} %get-tuple-element.26, f32[16,128,256]{2,1,0:T(8,128)} %get-tuple-element.27, ...), kind=kLoop, calls=%fused_computation.15 | loop fusion | flops 46137344 | bytes 24117248 | tf_op jit(solution)/shard_map/add | solution.py:143
  43.4 12.4 %copy.60 = f32[4,16,128,256]{3,0,2,1:T(4,128)} copy(f32[4,16,128,256]{3,2,1,0:T(8,128)} %multiply_add_fusion) | data formatting | bytes 16777216 | tf_op jit(solution)/shard_map/add | solution.py:143
  55.8 22.2 %gather_fusion = f32[2048,4,256]{2,1,0:T(4,128)} fusion(f32[4,2048,256]{2,0,1:T(4,128)} %bitcast.53, s32[2048]{0:T(1024)S(1)} %broadcast_clamp_fusion), kind=kCustom, calls=%fused_computation | custom fusion | bytes 16785408 | tf_op jit(solution)/shard_map/jit(_take)/gather | solution.py:80
  78.1 30.1 %multiply_reduce_fusion = f32[2048,4]{1,0:T(8,128)S(1)} fusion(f32[2048,4,256]{2,1,0:T(4,128)} %gather_fusion, f32[2048,256]{1,0:T(8,128)S(1)} %bitcast.54, pred[2048]{0:T(1024)(128)(4,1)S(1)} %compare_and_fusion), kind=kLoop, calls=%fused_computation.13 | loop fusion | flops 6283264 | bytes 10520576 | tf_op jit(solution)/shard_map/reduce_sum | solution.py:87
  108.6 1.0 fusion.1
  109.7 0.9 copy.64
  110.5 15.0 %all-to-all-start = ((f32[4,128,8]{2,0,1:T(4,128)}), f32[4,128,8]{2,0,1:T(4,128)S(1)}, u32[]{:S(2)}, u32[]{:S(2)}) async-start(f32[4,128,8]{2,0,1:T(4,128)} %copy.64), calls=%async_computation | async-start | bytes 524288 | tf_op jit(solution)/shard_map/all_to_all | solution.py:153
  125.5 2.3 %fusion.36 = (f32[4,1,128,256]{3,2,1,0:T(8,128)}, f32[4,1,128,256]{3,2,1,0:T(8,128)}) fusion(f32[4,16,128,256]{3,2,1,0:T(8,128)} %multiply_add_fusion), kind=kLoop, calls=%fused_computation.127 | loop fusion | bytes 2097152 | tf_op jit(solution)/shard_map/slice | solution.py:20
  127.8 1.1 collective-permute-start.2
  129.6 7.0 %all-to-all-done = f32[4,128,8]{2,0,1:T(4,128)S(1)} async-done(((f32[4,128,8]{2,0,1:T(4,128)}), f32[4,128,8]{2,0,1:T(4,128)S(1)}, u32[]{:S(2)}, u32[]{:S(2)}) %all-to-all-start) | async-done | bytes 16416 | tf_op jit(solution)/shard_map/all_to_all | solution.py:153
  138.5 0.9 copy.69
  139.4 7.4 %all-to-all-start.1 = ((f32[4,128,8]{2,0,1:T(4,128)}), f32[4,128,8]{2,0,1:T(4,128)S(1)}, u32[]{:S(2)}, u32[]{:S(2)}) async-start(f32[4,128,8]{2,0,1:T(4,128)} %copy.69), calls=%async_computation.1 | async-start | bytes 524288 | tf_op jit(solution)/shard_map/all_to_all | solution.py:155
  146.8 5.5 %slice_bitcast_fusion.2 = (f32[16,128,256]{2,1,0:T(8,128)S(1)}, f32[16,128,256]{2,1,0:T(8,128)}, f32[16,128,256]{2,1,0:T(8,128)}) fusion(f32[4,16,128,256]{3,2,1,0:T(8,128)} %multiply_add_fusion), kind=kLoop, calls=%fused_computation.18 | loop fusion | bytes 12582912 | tf_op jit(solution)/shard_map/mul | solution.py:43
  152.2 5.6 %all-to-all-done.1 = f32[4,128,8]{2,0,1:T(4,128)S(1)} async-done(((f32[4,128,8]{2,0,1:T(4,128)}), f32[4,128,8]{2,0,1:T(4,128)S(1)}, u32[]{:S(2)}, u32[]{:S(2)}) %all-to-all-start.1) | async-done | bytes 16416 | tf_op jit(solution)/shard_map/all_to_all | solution.py:155
  158.0 1.7 fusion
  159.7 28.5 %add_multiply_fusion = f32[4,16,128,256]{3,2,1,0:T(8,128)} fusion(f32[4,16,128,256]{3,2,1,0:T(8,128)} %param.8, f32[4,16,128,256]{3,2,1,0:T(8,128)} %multiply_add_fusion, f32[4,1,128,256]{3,2,1,0:T(8,128)S(1)} %collective-permute-done.2, f32[4,1,128,256]{3,2,1,0:T(8,128)} %collective-permute-done.3, f32[16,128,256]{2,1,0:T(8,128)} %get-tuple-element.22, ...), kind=kLoop, calls=%fused_computation.14 | loop fusion | flops 50331648 | bytes 32505856 | tf_op jit(solution)/shard_map/add | solution.py:144
  (65 shorter events, 5.5 us)
Async XLA Ops:
  2.9 14.3 %collective-permute-start = (f32[4,1,128,256]{3,2,1,0:T(8,128)}, f32[4,1,128,256]{3,2,1,0:T(8,128)S(1)}, u32[]{:S(2)}, u32[]{:S(2)}) collective-permute-start(f32[4,1,128,256]{3,2,1,0:T(8,128)} %get-tuple-element.29), channel_id=1, source_target_pairs={{1,0},{2,1},{3,2},{4,3},{5,4},{6,5},{7,6},{8,7},{9,8},{10,9},{11,1... | collective-permute-start | bytes 1572872 | tf_op jit(solution)/shard_map/ppermute | solution.py:25
  4.3 12.9 %collective-permute-start.1 = (f32[4,1,128,256]{3,2,1,0:T(8,128)}, f32[4,1,128,256]{3,2,1,0:T(8,128)}, u32[]{:S(2)}, u32[]{:S(2)}) collective-permute-start(f32[4,1,128,256]{3,2,1,0:T(8,128)} %get-tuple-element.28), channel_id=1, source_target_pairs={{0,1},{1,2},{2,3},{3,4},{4,5},{5,6},{6,7},{7,8},{8,9},{9,10},{10,1... | collective-permute-start | bytes 1572872 | tf_op jit(solution)/shard_map/ppermute | solution.py:23
  78.1 58.9 %copy-start = (f32[1024]{0:T(1024)S(1)}, f32[1024]{0:T(1024)}, u32[]{:S(2)}) copy-start(f32[1024]{0:T(1024)} %param.13) | copy-start | bytes 12292
  78.1 58.9 %copy-start.1 = (f32[1024]{0:T(1024)S(1)}, f32[1024]{0:T(1024)}, u32[]{:S(2)}) copy-start(f32[1024]{0:T(1024)} %param.15) | copy-start | bytes 12292
  78.1 60.2 %copy-start.2 = (f32[1024]{0:T(1024)S(1)}, f32[1024]{0:T(1024)}, u32[]{:S(2)}) copy-start(f32[1024]{0:T(1024)} %param.14) | copy-start | bytes 12292
  110.5 26.1 %all-to-all-start = ((f32[4,128,8]{2,0,1:T(4,128)}), f32[4,128,8]{2,0,1:T(4,128)S(1)}, u32[]{:S(2)}, u32[]{:S(2)}) async-start(f32[4,128,8]{2,0,1:T(4,128)} %copy.64), calls=%async_computation | async-start | bytes 524288 | tf_op jit(solution)/shard_map/all_to_all | solution.py:153
  127.8 31.9 %collective-permute-start.2 = (f32[4,1,128,256]{3,2,1,0:T(8,128)}, f32[4,1,128,256]{3,2,1,0:T(8,128)S(1)}, u32[]{:S(2)}, u32[]{:S(2)}) collective-permute-start(f32[4,1,128,256]{3,2,1,0:T(8,128)} %get-tuple-element.24), channel_id=1, source_target_pairs={{1,0},{2,1},{3,2},{4,3},{5,4},{6,5},{7,6},{8,7},{9,8},{10,9},{11,1... | collective-permute-start | bytes 1572872 | tf_op jit(solution)/shard_map/ppermute | solution.py:25
  128.9 30.8 %collective-permute-start.3 = (f32[4,1,128,256]{3,2,1,0:T(8,128)}, f32[4,1,128,256]{3,2,1,0:T(8,128)}, u32[]{:S(2)}, u32[]{:S(2)}) collective-permute-start(f32[4,1,128,256]{3,2,1,0:T(8,128)} %get-tuple-element.23), channel_id=1, source_target_pairs={{0,1},{1,2},{2,3},{3,4},{4,5},{5,6},{6,7},{7,8},{8,9},{9,10},{10,1... | collective-permute-start | bytes 1572872 | tf_op jit(solution)/shard_map/ppermute | solution.py:23
  139.4 18.5 %all-to-all-start.1 = ((f32[4,128,8]{2,0,1:T(4,128)}), f32[4,128,8]{2,0,1:T(4,128)S(1)}, u32[]{:S(2)}, u32[]{:S(2)}) async-start(f32[4,128,8]{2,0,1:T(4,128)} %copy.69), calls=%async_computation.1 | async-start | bytes 524288 | tf_op jit(solution)/shard_map/all_to_all | solution.py:155
where the time goes:
time: 189 us; the launch traced here: 188 us
  other arithmetic  90.7 us (48%)
  local copies, waits for them, and re-layouts  54.4 us (29%)
  starting transfers between devices  26.8 us (14%)
  waiting for transfers between devices  12.7 us (7%)
  matrix products  2.73 us (1%)
    reduce_sum x1, other arithmetic, sample_lines(): along_line = jnp.sum(picked * depth_weights[None, None], axis=3)  30.1 us
    add x1, other arithmetic, on_device(): 0.5 * state + 0.5 * (middle + time_step * transport(with_rims(middle)))  28.5 us
    add x1, other arithmetic, on_device(): middle = state + time_step * transport(with_rims(state))  26.2 us
    gather x1, local copies, waits for them, and re-layouts, sample_lines(): picked = jnp.take(lines, line_ids, axis=1).reshape(4, 4, points, line_cells)  22.2 us
    all_to_all x1, starting transfers between devices, on_device(): lax.all_to_all(outgoing, 'blk', split_axis=1, concat_axis=1, tiled=True)  15 us
    add x1, local copies, waits for them, and re-layouts, on_device(): middle = state + time_step * transport(with_rims(state))  12.4 us
    mul x2, local copies, waits for them, and re-layouts, transport(): velocity[0] * (east_side - west_side)  11.1 us
    all_to_all x1, starting transfers between devices, on_device(): lax.all_to_all(solved, 'blk', split_axis=1, concat_axis=1, tiled=True)  7.38 us
  transfers between devices with their start and end apart: 6, of which 2 were waited for; matrix products, arithmetic and copies ran while one was open for 13% of the time, Pallas kernels for 0%

commit v1 on v0

--- a/solution.py
+++ b/solution.py
@@ -152,7 +152,10 @@
     )
     incoming = lax.all_to_all(outgoing, "blk", split_axis=1, concat_axis=1, tiled=True)
     solved = wall_model(incoming, face_angles, face_height, wall_temp, face_visc)
-    returned = lax.all_to_all(solved, "blk", split_axis=1, concat_axis=1, tiled=True)
+    returned = jnp.concatenate(
+        lax.all_to_all(jnp.stack(jnp.split(solved, lax.axis_size("blk"), axis=1)), "blk", 0, 0),
+        axis=1,
+    )
     wall_flux = pick_slots(returned, slot_table)
     return (final_state, wall_flux)
 

time: 189 us -> 273 us (1.44)
  other arithmetic: 90.7 us -> 175 us
    unnamed x1 -> x128, other arithmetic: 0.02 us -> 82.3 us
  transfers between devices with their start and end apart: 6 -> 6, of which waited for: 2 -> 2; matrix products, arithmetic and copies ran while one was open for 13% -> 39% of each run, Pallas kernels for 0% -> 0%
where the time goes in v1:
time: 273 us; the launch traced here: 272 us
  other arithmetic  175 us (64%)
  local copies, waits for them, and re-layouts  54.5 us (20%)
  starting transfers between devices  26.8 us (10%)
  waiting for transfers between devices  12.7 us (5%)
  matrix products  2.73 us (1%)
    unnamed x128, other arithmetic  82.3 us
    reduce_sum x1, other arithmetic, sample_lines(): along_line = jnp.sum(picked * depth_weights[None, None], axis=3)  30.1 us
    add x1, other arithmetic, on_device(): 0.5 * state + 0.5 * (middle + time_step * transport(with_rims(middle)))  28.6 us
    add x1, other arithmetic, on_device(): middle = state + time_step * transport(with_rims(state))  26.3 us
    gather x1, local copies, waits for them, and re-layouts, sample_lines(): picked = jnp.take(lines, line_ids, axis=1).reshape(4, 4, points, line_cells)  22.2 us
    all_to_all x1, starting transfers between devices, on_device(): lax.all_to_all(outgoing, 'blk', split_axis=1, concat_axis=1, tiled=True)  15 us
    add x1, local copies, waits for them, and re-layouts, on_device(): middle = state + time_step * transport(with_rims(state))  12.4 us
    mul x2, local copies, waits for them, and re-layouts, transport(): velocity[0] * (east_side - west_side)  11.1 us
  transfers between devices with their start and end apart: 6, of which 2 were waited for; matrix products, arithmetic and copies ran while one was open for 39% of the time, Pallas kernels for 0%

profile of v1, /device:TPU:1, one launch (start us, length us, event | category | flops | bytes accessed | tf_op | source)
XLA Modules:
  0.0 272.2 jit_solution(80384556576318408)
XLA Ops:
  0.6 2.3 fusion.171
  2.9 1.4 collective-permute-start
  4.3 1.3 collective-permute-start.1
  5.6 0.7 broadcast_add_fusion.3
  6.4 0.8 subtract_multiply_fusion.1
  7.2 0.8 copy.332
  8.3 0.9 fusion.25
  10.4 1.7 slice_cosine_fusion
  13.0 5.6 %slice_bitcast_fusion.5 = (f32[16,128,256]{2,1,0:T(8,128)S(1)}, f32[16,128,256]{2,1,0:T(8,128)}, f32[16,128,256]{2,1,0:T(8,128)}) fusion(f32[4,16,128,256]{3,2,1,0:T(8,128)} %param.8), kind=kLoop, calls=%fused_computation.22 | loop fusion | bytes 12582912 | tf_op jit(solution)/shard_map/mul | solution.py:43
  18.6 26.3 %multiply_add_fusion = f32[4,16,128,256]{3,2,1,0:T(8,128)} fusion(f32[4,16,128,256]{3,2,1,0:T(8,128)} %param.8, f32[4,1,128,256]{3,2,1,0:T(8,128)S(1)} %collective-permute-done, f32[4,1,128,256]{3,2,1,0:T(8,128)} %collective-permute-done.1, f32[16,128,256]{2,1,0:T(8,128)} %get-tuple-element.27, f32[16,128,256]{2,1,0:T(8,128)} %get-tuple-element.28, ...), kind=kLoop, calls=%fused_computation.15 | loop fusion | flops 46137344 | bytes 24117248 | tf_op jit(solution)/shard_map/add | solution.py:143
  44.9 12.4 %copy.330 = f32[4,16,128,256]{3,0,2,1:T(4,128)} copy(f32[4,16,128,256]{3,2,1,0:T(8,128)} %multiply_add_fusion) | data formatting | bytes 16777216 | tf_op jit(solution)/shard_map/add | solution.py:143
  57.2 22.2 %gather_fusion = f32[2048,4,256]{2,1,0:T(4,128)} fusion(f32[4,2048,256]{2,0,1:T(4,128)} %bitcast.441, s32[2048]{0:T(1024)S(1)} %broadcast_clamp_fusion), kind=kCustom, calls=%fused_computation | custom fusion | bytes 16785408 | tf_op jit(solution)/shard_map/jit(_take)/gather | solution.py:80
  79.6 30.1 %multiply_reduce_fusion = f32[2048,4]{1,0:T(8,128)S(1)} fusion(f32[2048,4,256]{2,1,0:T(4,128)} %gather_fusion, f32[2048,256]{1,0:T(8,128)S(1)} %bitcast.442, pred[2048]{0:T(1024)(128)(4,1)S(1)} %compare_and_fusion), kind=kLoop, calls=%fused_computation.13 | loop fusion | flops 6283264 | bytes 10520576 | tf_op jit(solution)/shard_map/reduce_sum | solution.py:87
  110.1 1.0 fusion.1
  111.2 0.9 copy.334
  112.0 15.0 %all-to-all-start = ((f32[4,128,8]{2,0,1:T(4,128)}), f32[4,128,8]{2,0,1:T(4,128)S(1)}, u32[]{:S(2)}, u32[]{:S(2)}) async-start(f32[4,128,8]{2,0,1:T(4,128)} %copy.334), calls=%async_computation | async-start | bytes 524288 | tf_op jit(solution)/shard_map/all_to_all | solution.py:153
  127.0 2.3 fusion.170
  129.3 1.1 collective-permute-start.2
  131.0 7.0 %all-to-all-done = f32[4,128,8]{2,0,1:T(4,128)S(1)} async-done(((f32[4,128,8]{2,0,1:T(4,128)}), f32[4,128,8]{2,0,1:T(4,128)S(1)}, u32[]{:S(2)}, u32[]{:S(2)}) %all-to-all-start) | async-done | bytes 16416 | tf_op jit(solution)/shard_map/all_to_all | solution.py:153
  223.2 7.4 %all-to-all-start.1 = ((f32[128,4,8]{2,1,0:T(4,128)}), f32[128,4,8]{2,1,0:T(4,128)S(1)}, u32[]{:S(2)}, u32[]{:S(2)}) async-start(f32[128,4,8]{2,1,0:T(4,128)} %constant_dynamic-update-slice_fusion), calls=%async_computation.1 | async-start | bytes 524288 | tf_op jit(solution)/shard_map/all_to_all | solution.py:156
  230.5 5.5 %slice_bitcast_fusion.2 = (f32[16,128,256]{2,1,0:T(8,128)S(1)}, f32[16,128,256]{2,1,0:T(8,128)}, f32[16,128,256]{2,1,0:T(8,128)}) fusion(f32[4,16,128,256]{3,2,1,0:T(8,128)} %multiply_add_fusion), kind=kLoop, calls=%fused_computation.18 | loop fusion | bytes 12582912 | tf_op jit(solution)/shard_map/mul | solution.py:43
  236.0 5.6 %all-to-all-done.1 = f32[128,4,8]{2,1,0:T(4,128)S(1)} async-done(((f32[128,4,8]{2,1,0:T(4,128)}), f32[128,4,8]{2,1,0:T(4,128)S(1)}, u32[]{:S(2)}, u32[]{:S(2)}) %all-to-all-start.1) | async-done | bytes 16416 | tf_op jit(solution)/shard_map/all_to_all | solution.py:156
  241.8 1.7 fusion
  243.5 28.6 %add_multiply_fusion = f32[4,16,128,256]{3,2,1,0:T(8,128)} fusion(f32[4,16,128,256]{3,2,1,0:T(8,128)} %param.8, f32[4,16,128,256]{3,2,1,0:T(8,128)} %multiply_add_fusion, f32[4,1,128,256]{3,2,1,0:T(8,128)S(1)} %collective-permute-done.2, f32[4,1,128,256]{3,2,1,0:T(8,128)} %collective-permute-done.3, f32[16,128,256]{2,1,0:T(8,128)} %get-tuple-element.23, ...), kind=kLoop, calls=%fused_computation.14 | loop fusion | flops 50331648 | bytes 32505856 | tf_op jit(solution)/shard_map/add | solution.py:144
  (194 shorter events, 88.7 us)
Async XLA Ops:
  2.9 15.7 %collective-permute-start = (f32[4,1,128,256]{3,2,1,0:T(8,128)}, f32[4,1,128,256]{3,2,1,0:T(8,128)S(1)}, u32[]{:S(2)}, u32[]{:S(2)}) collective-permute-start(f32[4,1,128,256]{3,2,1,0:T(8,128)} %get-tuple-element.30), channel_id=1, source_target_pairs={{1,0},{2,1},{3,2},{4,3},{5,4},{6,5},{7,6},{8,7},{9,8},{10,9},{11,1... | collective-permute-start | bytes 1572872 | tf_op jit(solution)/shard_map/ppermute | solution.py:25
  4.3 14.3 %collective-permute-start.1 = (f32[4,1,128,256]{3,2,1,0:T(8,128)}, f32[4,1,128,256]{3,2,1,0:T(8,128)}, u32[]{:S(2)}, u32[]{:S(2)}) collective-permute-start(f32[4,1,128,256]{3,2,1,0:T(8,128)} %get-tuple-element.29), channel_id=1, source_target_pairs={{0,1},{1,2},{2,3},{3,4},{4,5},{5,6},{6,7},{7,8},{8,9},{9,10},{10,1... | collective-permute-start | bytes 1572872 | tf_op jit(solution)/shard_map/ppermute | solution.py:23
  79.6 58.9 %copy-start = (f32[1024]{0:T(1024)S(1)}, f32[1024]{0:T(1024)}, u32[]{:S(2)}) copy-start(f32[1024]{0:T(1024)} %param.13) | copy-start | bytes 12292
  79.6 58.9 %copy-start.1 = (f32[1024]{0:T(1024)S(1)}, f32[1024]{0:T(1024)}, u32[]{:S(2)}) copy-start(f32[1024]{0:T(1024)} %param.15) | copy-start | bytes 12292
  79.6 60.4 %copy-start.2 = (f32[1024]{0:T(1024)S(1)}, f32[1024]{0:T(1024)}, u32[]{:S(2)}) copy-start(f32[1024]{0:T(1024)} %param.14) | copy-start | bytes 12292
  112.0 26.1 %all-to-all-start = ((f32[4,128,8]{2,0,1:T(4,128)}), f32[4,128,8]{2,0,1:T(4,128)S(1)}, u32[]{:S(2)}, u32[]{:S(2)}) async-start(f32[4,128,8]{2,0,1:T(4,128)} %copy.334), calls=%async_computation | async-start | bytes 524288 | tf_op jit(solution)/shard_map/all_to_all | solution.py:153
  129.3 114.2 %collective-permute-start.2 = (f32[4,1,128,256]{3,2,1,0:T(8,128)}, f32[4,1,128,256]{3,2,1,0:T(8,128)S(1)}, u32[]{:S(2)}, u32[]{:S(2)}) collective-permute-start(f32[4,1,128,256]{3,2,1,0:T(8,128)} %get-tuple-element.25), channel_id=1, source_target_pairs={{1,0},{2,1},{3,2},{4,3},{5,4},{6,5},{7,6},{8,7},{9,8},{10,9},{11,1... | collective-permute-start | bytes 1572872 | tf_op jit(solution)/shard_map/ppermute | solution.py:25
  130.4 113.1 %collective-permute-start.3 = (f32[4,1,128,256]{3,2,1,0:T(8,128)}, f32[4,1,128,256]{3,2,1,0:T(8,128)}, u32[]{:S(2)}, u32[]{:S(2)}) collective-permute-start(f32[4,1,128,256]{3,2,1,0:T(8,128)} %get-tuple-element.24), channel_id=1, source_target_pairs={{0,1},{1,2},{2,3},{3,4},{4,5},{5,6},{6,7},{7,8},{8,9},{9,10},{10,1... | collective-permute-start | bytes 1572872 | tf_op jit(solution)/shard_map/ppermute | solution.py:23
  223.2 18.5 %all-to-all-start.1 = ((f32[128,4,8]{2,1,0:T(4,128)}), f32[128,4,8]{2,1,0:T(4,128)S(1)}, u32[]{:S(2)}, u32[]{:S(2)}) async-start(f32[128,4,8]{2,1,0:T(4,128)} %constant_dynamic-update-slice_fusion), calls=%async_computation.1 | async-start | bytes 524288 | tf_op jit(solution)/shard_map/all_to_all | solution.py:156
